TPU v7x, 32 devices: a whole 2x2x4 slice. The times are simulated.
32 devices in a mesh: inst: 8 (over z, y), space: 4 (over x, core).
Axes of the slice: x: 2, y: 2, z: 4, core: 2. Of those that a mesh axis runs over, the one named last changes fastest.
Arguments:
- state: float32 [32, 320, 512], P('inst', None, 'space'), may hold values from -6 to 6
- forcing: float32 [32, 320, 512], P('inst', None, 'space'), may hold values from -6 to 6
- flux_jac: float32 [3, 5, 5], replicated, may hold values from -0.875 to 0.875
- jacobi_inv: float32 [32, 320, 320], P('inst'), may hold values from -0.01 to 0.03
- cross_nbr: int32 [4, 64], replicated, may hold values from 0 to 63, as said below
- lower_match: int32 [32, 4, 64], P('inst', 'space'), may hold values from 0 to 63, as said below
Outputs:
- residual: float32 [32, 320, 512], P('inst', None, 'space')
- updated: float32 [32, 320, 512], P('inst', None, 'space')
Inputs may be any that keep to these rules, and one draw needn't show every extreme that they name: `cross_nbr`: the cells form a grid of 8 by 8, periodic in both directions, in an order drawn from the seed; if row 0 names n for cell c then row 1 names c for n, and likewise rows 2 and 3. lower_match[t, p] is the identity except at the sliding interface p = 4 // 2, where it is the cyclic pitch shift of the cross_nbr grid by (t * 8 // 32 + r) % 8 rows, with one offset r drawn from the seed: the cell below that faces c is the one reached from c by that many steps through row 1 of cross_nbr.
All inputs are finite; a program needn't handle non-finite values.
Results may differ from a plain program's by a relative error of at most 0.0003.
Values sent between devices are 32-bit elements; how exact they have to be, the bound alone decides.
A program may use at most 128 MiB of HBM per device.

v0:
```python
import math
import jax
import jax.numpy as jnp
import numpy as np
from jax import lax
from jax.sharding import PartitionSpec as P

VARS = 5
NODE1 = 4
PITCH_ELEMENTS = 8
EZ = 8
SWEEPS = 2
dissipation = 0.6
frequency = 0.25


def with_halo(block, sides, width):
    for axis, dim in sides:
        count = lax.axis_size(axis)
        forward = [(i, i + 1) for i in range(count - 1)]
        backward = [(target, source) for source, target in forward]
        low = lax.ppermute(
            lax.slice_in_dim(block, block.shape[dim] - width, None, axis=dim), axis, forward
        )
        high = lax.ppermute(lax.slice_in_dim(block, 0, width, axis=dim), axis, backward)
        block = jnp.concatenate([low, block, high], axis=dim)
    return block


def lobatto_derivative(count_of_nodes):
    inner_point = math.sqrt(0.2)
    points = np.array([-1.0, -inner_point, inner_point, 1.0])
    barycentric = np.ones(count_of_nodes)
    for first_index in range(count_of_nodes):
        for second_index in range(count_of_nodes):
            if first_index != second_index:
                barycentric[first_index] = barycentric[first_index] / (
                    points[first_index] - points[second_index]
                )
    table = np.zeros((count_of_nodes, count_of_nodes))
    for first_index in range(count_of_nodes):
        for second_index in range(count_of_nodes):
            if first_index != second_index:
                table[first_index, second_index] = (
                    barycentric[second_index]
                    / barycentric[first_index]
                    / (points[first_index] - points[second_index])
                )
        table[first_index, first_index] = -np.sum(table[first_index])
    return table


def time_matrix(count):
    pitch_offset = (
        jnp.arange(count, dtype=jnp.int32)[:, None] - jnp.arange(count, dtype=jnp.int32)[None, :]
    )
    parity = 1.0 - 2.0 * (pitch_offset % 2).astype(jnp.float32)
    angle = jnp.pi * pitch_offset.astype(jnp.float32) / count
    safe_tan = jnp.where(pitch_offset == 0, 1.0, jnp.tan(angle))
    return jnp.where(pitch_offset == 0, 0.0, 0.5 * frequency * parity / safe_tan)


def differentiate(stack):
    matrix = time_matrix(stack.shape[0])
    return jnp.einsum("ts,sbe->tbe", matrix, stack, precision=lax.Precision.HIGHEST)


def time_rates(field):
    return lax.all_to_all(
        differentiate(lax.all_to_all(field, "inst", split_axis=2, concat_axis=0, tiled=True)),
        "inst",
        split_axis=0,
        concat_axis=2,
        tiled=True,
    )


def permute_cells(values, index):
    return jnp.take_along_axis(values, index[:, None, :], axis=2)


def face_term(plus, minus, jacobian, sign):
    matrix = sign * jacobian - dissipation * jnp.eye(jacobian.shape[0], dtype=jnp.float32)
    return jnp.einsum("wv,tvabe->twabe", matrix, plus - minus, precision=lax.Precision.HIGHEST)


def space_residual(field, flux_jac, derivative, neighbours, matching_cells, inverse_cells):
    local_times, block, elements = field.shape
    nodes = NODE1
    width = VARS
    cells = PITCH_ELEMENTS * EZ
    face_size = width * nodes * nodes
    highest = lax.Precision.HIGHEST
    reshaped_array = field.reshape(local_times, width, nodes, nodes, nodes, elements)
    low_x = reshaped_array[:, :, 0]
    high_x = reshaped_array[:, :, nodes - 1]
    first_trace = low_x[..., :cells].reshape(local_times, face_size, cells)
    last_trace = high_x[..., elements - cells :].reshape(local_times, face_size, cells)
    outgoing = jnp.concatenate([permute_cells(first_trace, inverse_cells), last_trace], axis=2)
    received = with_halo(outgoing, (("space", 2),), cells)
    from_below = received[:, :, :cells]
    from_above = received[:, :, 3 * cells :]
    from_below = permute_cells(from_below, matching_cells).reshape(
        local_times, width, nodes, nodes, cells
    )
    from_above = from_above.reshape(local_times, width, nodes, nodes, cells)
    plus_low_x = jnp.concatenate([from_below, high_x[..., : elements - cells]], axis=4)
    plus_high_x = jnp.concatenate([low_x[..., cells:], from_above], axis=4)
    along_x = jnp.einsum("ai,tvijke->tvajke", derivative, reshaped_array, precision=highest)
    along_y = jnp.einsum("aj,tvijke->tviake", derivative, reshaped_array, precision=highest)
    along_z = jnp.einsum("ak,tvijke->tvijae", derivative, reshaped_array, precision=highest)
    volume = jnp.einsum("wv,tvijke->twijke", flux_jac[0], along_x, precision=highest)
    volume = volume + jnp.einsum("wv,tvijke->twijke", flux_jac[1], along_y, precision=highest)
    volume = volume + jnp.einsum("wv,tvijke->twijke", flux_jac[2], along_z, precision=highest)
    scale = nodes * (nodes - 1) / 4.0
    low_y = reshaped_array[:, :, :, 0]
    high_y = reshaped_array[:, :, :, nodes - 1]
    low_z = reshaped_array[:, :, :, :, 0]
    high_z = reshaped_array[:, :, :, :, nodes - 1]
    volume = volume.at[:, :, 0].add(scale * face_term(plus_low_x, low_x, flux_jac[0], -1.0))
    volume = volume.at[:, :, nodes - 1].add(
        scale * face_term(plus_high_x, high_x, flux_jac[0], 1.0)
    )
    volume = volume.at[:, :, :, 0].add(
        scale * face_term(jnp.take(high_y, neighbours[0], axis=4), low_y, flux_jac[1], -1.0)
    )
    volume = volume.at[:, :, :, nodes - 1].add(
        scale * face_term(jnp.take(low_y, neighbours[1], axis=4), high_y, flux_jac[1], 1.0)
    )
    volume = volume.at[:, :, :, :, 0].add(
        scale * face_term(jnp.take(high_z, neighbours[2], axis=4), low_z, flux_jac[2], -1.0)
    )
    volume = volume.at[:, :, :, :, nodes - 1].add(
        scale * face_term(jnp.take(low_z, neighbours[3], axis=4), high_z, flux_jac[2], 1.0)
    )
    return volume.reshape(local_times, block, elements)


def body(state, forcing, flux_jac, jacobi_inv, cross_nbr, lower_match):
    local_times, block, elements = state.shape
    cells = PITCH_ELEMENTS * EZ
    derivative = jnp.asarray(lobatto_derivative(NODE1), jnp.float32)
    layer_start = jnp.arange(elements // cells, dtype=jnp.int32) * cells
    neighbours = (layer_start[None, :, None] + cross_nbr[:, None, :]).reshape(4, elements)
    matching_cells = lower_match[:, 0, :]
    inverse_cells = jnp.argsort(matching_cells, axis=-1)
    current = state
    first_residual = state
    for sweep in range(SWEEPS):
        rates = time_rates(current)
        spatial = space_residual(
            current, flux_jac, derivative, neighbours, matching_cells, inverse_cells
        )
        residual = spatial + rates - forcing
        if sweep == 0:
            first_residual = residual
        current = current - jnp.einsum(
            "tpq,tqe->tpe", jacobi_inv, residual, precision=lax.Precision.HIGHEST
        )
    return (first_residual, current)


def solution(mesh):
    return jax.shard_map(
        body,
        mesh=mesh,
        in_specs=(
            P("inst", None, "space"),
            P("inst", None, "space"),
            P(),
            P("inst", None, None),
            P(),
            P("inst", "space", None),
        ),
        out_specs=(P("inst", None, "space"), P("inst", None, "space")),
        check_vma=False,
    )
```

profile of v0, /device:TPU:1, one launch (start us, length us, event | category | flops | bytes accessed | tf_op | source)
XLA Modules:
  0.0 344.2 jit_solution(9277258930535717636)
XLA Ops:
  10.9 4.5 %collective-permute-start = (f32[4,80,64]{1,2,0:T(8,128)}, f32[4,80,64]{1,2,0:T(8,128)S(1)}, u32[]{:S(2)}, u32[]{:S(2)}) collective-permute-start(f32[4,80,64]{1,2,0:T(8,128)} %copy.324), channel_id=1, source_target_pairs={{0,1},{1,2},{2,3},{4,5},{5,6},{6,7},{8,9},{9,10},{10,11},{12,13},{... | collective-permute-start | bytes 245768 | tf_op jit(solution)/shard_map/ppermute | solution.py:22
  16.5 6.1 %all-to-all-start = ((f32[4,320,128]{1,0,2:T(4,128)}), f32[4,320,128]{1,0,2:T(4,128)}, u32[]{:S(2)}, u32[]{:S(2)}) async-start(f32[4,320,128]{1,0,2:T(4,128)} %copy.355), calls=%async_computation | async-start | bytes 1572864 | tf_op jit(solution)/shard_map/all_to_all | solution.py:70
  30.4 4.5 %copy.455 = f32[4,5,4,4,1,128]{1,3,2,0,5,4:T(4,128)} copy(f32[4,5,4,4,1,128]{5,4,3,2,1,0:T(1,128)} %get-tuple-element.160) | data formatting | bytes 327680
  34.9 4.3 %copy.463 = f32[4,5,4,4,1,128]{1,3,5,2,0,4:T(4,128)} copy(f32[4,5,4,4,1,128]{5,4,3,2,1,0:T(1,128)} %get-tuple-element.160) | data formatting | bytes 327680 | tf_op jit(solution)/shard_map/squeeze | solution.py:118
  39.2 2.4 fusion.145
  41.7 2.4 convolution_add_fusion.3
  46.5 4.6 %copy.451 = f32[4,5,4,1,4,128]{1,4,2,0,5,3:T(4,128)} copy(f32[4,5,4,1,4,128]{5,4,3,2,1,0:T(4,128)} %get-tuple-element.162) | data formatting | bytes 327680
  51.1 4.3 %copy.450 = f32[4,5,4,1,4,128]{1,4,5,2,0,3:T(4,128)} copy(f32[4,5,4,1,4,128]{5,4,3,2,1,0:T(4,128)} %get-tuple-element.163) | data formatting | bytes 327680
  55.4 3.2 copy.342
  58.6 3.3 copy.454
  61.9 7.7 %gather_fusion.2 = f32[128,4,5,4,4]{2,4,3,1,0:T(4,128)} fusion(f32[4,5,4,4,128]{1,3,4,2,0:T(4,128)} %bitcast.450, s32[1024]{0:T(1024)S(1)} %pad_clamp_fusion.3), kind=kCustom, calls=%fused_computation.1.clone | custom fusion | bytes 328192 | tf_op jit(solution)/shard_map/jit(_take)/gather | solution.py:125
  69.6 7.7 %gather_fusion.3 = f32[128,4,5,4,4]{2,4,3,1,0:T(4,128)} fusion(f32[4,5,4,4,128]{1,3,4,2,0:T(4,128)} %copy.342, s32[1024]{0:T(1024)S(1)} %pad_clamp_fusion.2), kind=kCustom, calls=%fused_computation.5.clone | custom fusion | bytes 328192 | tf_op jit(solution)/shard_map/jit(_take)/gather | solution.py:128
  77.4 6.0 %bitcast_subtract_fusion.6 = f32[4,5,4,4,128]{1,3,4,2,0:T(4,128)} fusion(f32[128,4,5,4,4]{2,4,3,1,0:T(4,128)} %gather_fusion.3, pred[128]{0:T(512)(128)(4,1)S(1)} %get-tuple-element.189, f32[4,5,4,1,4,128]{1,4,5,2,0,3:T(4,128)} %copy.450), kind=kLoop, calls=%fused_computation.22 | loop fusion | flops 81920 | bytes 491648 | tf_op jit(solution)/shard_map/sub | solution.py:84
  83.3 7.8 %gather_fusion.4 = f32[128,4,5,4,4]{2,4,3,1,0:T(4,128)} fusion(f32[4,5,4,4,128]{1,3,4,2,0:T(4,128)} %bitcast.451, s32[1024]{0:T(1024)S(1)} %pad_clamp_fusion.1), kind=kCustom, calls=%fused_computation.6.clone | custom fusion | bytes 328192 | tf_op jit(solution)/shard_map/jit(_take)/gather | solution.py:131
  91.1 7.7 %gather_fusion.5 = f32[128,4,5,4,4]{2,4,3,1,0:T(4,128)} fusion(f32[4,5,4,4,128]{1,3,4,2,0:T(4,128)} %bitcast.455, s32[1024]{0:T(1024)S(1)} %pad_clamp_fusion), kind=kCustom, calls=%fused_computation.7.clone | custom fusion | bytes 328192 | tf_op jit(solution)/shard_map/jit(_take)/gather | solution.py:134
  98.8 5.9 %bitcast_subtract_fusion.4 = f32[4,5,4,4,128]{1,3,4,2,0:T(4,128)} fusion(f32[128,4,5,4,4]{2,4,3,1,0:T(4,128)} %gather_fusion.5, pred[128]{0:T(512)(128)(4,1)S(1)} %get-tuple-element.187, f32[4,5,4,4,1,128]{1,3,5,2,0,4:T(4,128)} %copy.454), kind=kLoop, calls=%fused_computation.20 | loop fusion | flops 81920 | bytes 491648 | tf_op jit(solution)/shard_map/sub | solution.py:84
  106.3 3.1 bitcast_subtract_fusion.7
  111.3 3.5 %bitcast_subtract_fusion.5 = f32[4,5,4,4,128]{1,3,2,0,4:T(4,128)} fusion(f32[4,5,4,4,1,128]{1,3,2,0,5,4:T(4,128)S(1)} %copy-done.7, f32[128,4,5,4,4]{2,4,3,1,0:T(4,128)S(1)} %copy-done.13, pred[128]{0:T(512)(128)(4,1)S(1)} %get-tuple-element.188), kind=kLoop, calls=%fused_computation.21 | loop fusion | flops 81920 | bytes 491648 | tf_op jit(solution)/shard_map/sub | solution.py:84
  124.3 6.9 %fusion.126 = f32[4,5,4,4,4,128]{5,1,4,3,2,0:T(8,128)} fusion(f32[4,5,4,4,4,128]{5,1,4,3,2,0:T(8,128)} %fusion.134, f32[4,5,4,1,4,128]{5,1,4,2,0,3:T(8,128)S(1)} %slice_bitcast_fusion.2, f32[4,5,4,4,128]{1,3,2,0,4:T(4,128)S(1)} %copy-done.8, f32[1,5,5]{2,0,1:T(1,128)S(1)} %get-tuple-element.177), kind=kOutput, calls=%fused_computation.98 | convolution fusion | flops 2539620 | bytes 589924 | tf_op jit(solution)/shard_map/wv,tvabe->twabe/dot_general | solution.py:84
  139.1 5.6 %all-to-all-start.1 = ((f32[32,320,16]{1,2,0:T(8,128)}), f32[32,320,16]{1,2,0:T(8,128)S(1)}, u32[]{:S(2)}, u32[]{:S(2)}) async-start(f32[32,320,16]{1,2,0:T(8,128)} %copy.358), calls=%async_computation.1 | async-start | bytes 1572864 | tf_op jit(solution)/shard_map/all_to_all | solution.py:69
  144.7 6.8 %fusion.117 = f32[4,5,4,4,4,128]{5,1,4,3,2,0:T(8,128)} fusion(f32[4,5,4,4,4,128]{5,1,4,3,2,0:T(8,128)} %fusion.126, f32[4,5,4,1,4,128]{5,1,4,2,0,3:T(8,128)} %slice_bitcast_fusion.1, f32[4,5,4,4,128]{1,3,4,2,0:T(4,128)} %bitcast_subtract_fusion.6, f32[1,5,5]{2,0,1:T(1,128)S(1)} %get-tuple-element.177), kind=kOutput, calls=%fused_computation.95 | convolution fusion | flops 2539595 | bytes 4718692 | tf_op jit(solution)/shard_map/wv,tvabe->twabe/dot_general | solution.py:84
  152.5 8.9 %fusion.108 = f32[4,5,4,4,4,128]{5,1,4,3,2,0:T(8,128)} fusion(f32[4,5,4,4,4,128]{5,1,4,3,2,0:T(8,128)} %fusion.117, f32[4,5,4,4,1,128]{5,1,3,2,0,4:T(8,128)S(1)} %slice_bitcast_fusion, f32[4,5,4,4,128]{1,3,2,0,4:T(4,128)} %bitcast_subtract_fusion.5, f32[1,5,5]{2,0,1:T(1,128)S(1)} %get-tuple-element.176), kind=kOutput, calls=%fused_computation.92 | convolution fusion | flops 2539620 | bytes 4620388 | tf_op jit(solution)/shard_map/wv,tvabe->twabe/dot_general | solution.py:84
  161.4 5.6 %fusion.99 = f32[4,5,4,4,4,128]{5,1,4,3,2,0:T(8,128)} fusion(f32[4,5,4,4,4,128]{5,1,4,3,2,0:T(8,128)} %fusion.108, f32[4,5,4,4,128]{1,3,4,2,0:T(4,128)S(1)} %copy-done.4, f32[1,5,5]{2,0,1:T(1,128)S(1)} %get-tuple-element.176), kind=kOutput, calls=%fused_computation.89 | convolution fusion | flops 2539595 | bytes 688228 | tf_op jit(solution)/shard_map/wv,tvabe->twabe/dot_general | solution.py:84
  183.0 3.4 copy.461
  186.4 3.2 copy.465
  202.3 3.7 %collective-permute-start.2 = (f32[4,80,64]{1,2,0:T(8,128)S(1)}, f32[4,80,64]{1,2,0:T(8,128)S(1)}, u32[]{:S(2)}, u32[]{:S(2)}) collective-permute-start(f32[4,80,64]{1,2,0:T(8,128)S(1)} %copy.370), channel_id=1, source_target_pairs={{0,1},{1,2},{2,3},{4,5},{5,6},{6,7},{8,9},{9,10},{10,11},{12,13},{... | collective-permute-start | bytes 245768 | tf_op jit(solution)/shard_map/ppermute | solution.py:22
  206.0 3.8 %copy.459 = f32[4,5,4,1,4,128]{1,4,2,0,5,3:T(4,128)} copy(f32[4,5,4,1,4,128]{5,4,3,2,1,0:T(4,128)S(1)} %copy-done.23) | data formatting | bytes 327680
  209.8 3.2 copy.458
  212.9 7.7 %gather_fusion.8 = f32[128,4,5,4,4]{2,4,3,1,0:T(4,128)} fusion(f32[4,5,4,4,128]{1,3,4,2,0:T(4,128)} %bitcast.452, s32[1024]{0:T(1024)S(1)} %pad_clamp_fusion.3), kind=kCustom, calls=%fused_computation.8.clone | custom fusion | bytes 328192 | tf_op jit(solution)/shard_map/jit(_take)/gather | solution.py:125
  220.7 3.1 copy.386
  223.8 7.8 %gather_fusion.9 = f32[128,4,5,4,4]{2,4,3,1,0:T(4,128)} fusion(f32[4,5,4,4,128]{1,3,4,2,0:T(4,128)} %copy.386, s32[1024]{0:T(1024)S(1)} %pad_clamp_fusion.2), kind=kCustom, calls=%fused_computation.9.clone | custom fusion | bytes 328192 | tf_op jit(solution)/shard_map/jit(_take)/gather | solution.py:128
  231.5 5.8 %bitcast_subtract_fusion.2 = f32[4,5,4,4,128]{1,3,4,2,0:T(4,128)} fusion(f32[128,4,5,4,4]{2,4,3,1,0:T(4,128)} %gather_fusion.9, pred[128]{0:T(512)(128)(4,1)S(1)} %get-tuple-element.189, f32[4,5,4,1,4,128]{1,4,5,2,0,3:T(4,128)} %copy.458), kind=kLoop, calls=%fused_computation.16 | loop fusion | flops 81920 | bytes 491648 | tf_op jit(solution)/shard_map/sub | solution.py:84
  237.3 3.3 copy.460
  240.6 7.8 %gather_fusion.10 = f32[128,4,5,4,4]{2,4,3,1,0:T(4,128)} fusion(f32[4,5,4,4,128]{1,3,4,2,0:T(4,128)} %bitcast.453, s32[1024]{0:T(1024)S(1)} %pad_clamp_fusion.1), kind=kCustom, calls=%fused_computation.10.clone | custom fusion | bytes 328192 | tf_op jit(solution)/shard_map/jit(_take)/gather | solution.py:131
  248.4 7.7 %gather_fusion.11 = f32[128,4,5,4,4]{2,4,3,1,0:T(4,128)} fusion(f32[4,5,4,4,128]{1,3,4,2,0:T(4,128)} %bitcast.454, s32[1024]{0:T(1024)S(1)} %pad_clamp_fusion), kind=kCustom, calls=%fused_computation.11.clone | custom fusion | bytes 328192 | tf_op jit(solution)/shard_map/jit(_take)/gather | solution.py:134
  256.1 5.8 %bitcast_subtract_fusion = f32[4,5,4,4,128]{1,3,4,2,0:T(4,128)} fusion(f32[128,4,5,4,4]{2,4,3,1,0:T(4,128)} %gather_fusion.11, pred[128]{0:T(512)(128)(4,1)S(1)} %get-tuple-element.187, f32[4,5,4,4,1,128]{1,3,5,2,0,4:T(4,128)} %copy.460), kind=kLoop, calls=%fused_computation.12 | loop fusion | flops 81920 | bytes 491648 | tf_op jit(solution)/shard_map/sub | solution.py:84
  261.9 6.0 %all-to-all-start.2 = ((f32[4,320,128]{1,0,2:T(4,128)}), f32[4,320,128]{1,0,2:T(4,128)}, u32[]{:S(2)}, u32[]{:S(2)}) async-start(f32[4,320,128]{1,0,2:T(4,128)} %copy.398), calls=%async_computation.2 | async-start | bytes 1572864 | tf_op jit(solution)/shard_map/all_to_all | solution.py:70
  267.9 2.8 convolution_add_fusion.1
  270.7 5.8 %bitcast_subtract_fusion.3 = f32[4,5,4,4,128]{1,3,2,0,4:T(4,128)} fusion(f32[4,5,4,1,4,128]{1,4,2,0,5,3:T(4,128)} %copy.459, f32[128,4,5,4,4]{2,4,3,1,0:T(4,128)} %gather_fusion.8, pred[128]{0:T(512)(128)(4,1)S(1)} %get-tuple-element.190), kind=kLoop, calls=%fused_computation.19 | loop fusion | flops 81920 | bytes 491648 | tf_op jit(solution)/shard_map/sub | solution.py:84
  278.1 3.1 bitcast_subtract_fusion.1
  281.2 2.4 fusion.16
  299.2 5.8 %all-to-all-start.3 = ((f32[32,320,16]{1,2,0:T(8,128)}), f32[32,320,16]{1,2,0:T(8,128)}, u32[]{:S(2)}, u32[]{:S(2)}) async-start(f32[32,320,16]{1,2,0:T(8,128)} %copy.401), calls=%async_computation.3 | async-start | bytes 1572864 | tf_op jit(solution)/shard_map/all_to_all | solution.py:69
  305.1 9.1 %fusion.81 = f32[4,5,4,4,4,128]{5,1,3,2,0,4:T(8,128)} fusion(f32[4,5,4,4,4,128]{5,1,3,2,0,4:T(8,128)} %fusion.138, f32[4,5,4,4,128]{1,3,2,0,4:T(4,128)} %bitcast_subtract_fusion.3, f32[1,5,5]{2,0,1:T(1,128)S(1)} %get-tuple-element.177), kind=kOutput, calls=%fused_computation.83 | convolution fusion | flops 2539620 | bytes 4718692 | tf_op jit(solution)/shard_map/wv,tvabe->twabe/dot_general | solution.py:84
  314.2 5.6 %fusion.75 = f32[4,5,4,4,4,128]{5,1,3,2,0,4:T(8,128)} fusion(f32[4,5,4,4,4,128]{5,1,3,2,0,4:T(8,128)} %fusion.81, f32[4,5,4,4,128]{1,3,4,2,0:T(4,128)S(1)} %copy-done.2, f32[1,5,5]{2,0,1:T(1,128)S(1)} %get-tuple-element.177), kind=kOutput, calls=%fused_computation.81 | convolution fusion | flops 2539595 | bytes 688228 | tf_op jit(solution)/shard_map/wv,tvabe->twabe/dot_general | solution.py:84
  319.8 7.9 %fusion.93 = f32[4,5,4,4,4,128]{5,1,3,2,0,4:T(8,128)} fusion(f32[4,5,4,4,4,128]{5,1,3,2,0,4:T(8,128)} %fusion.75, f32[4,5,4,4,128]{1,3,2,0,4:T(4,128)S(1)} %copy-done.6, f32[1,5,5]{2,0,1:T(1,128)S(1)} %get-tuple-element.176), kind=kOutput, calls=%fused_computation.87 | convolution fusion | flops 2539620 | bytes 688228 | tf_op jit(solution)/shard_map/wv,tvabe->twabe/dot_general | solution.py:84
  327.7 5.5 %fusion.87 = f32[4,5,4,4,4,128]{5,1,3,2,0,4:T(8,128)} fusion(f32[4,5,4,4,4,128]{5,1,3,2,0,4:T(8,128)} %fusion.93, f32[4,5,4,4,128]{1,3,4,2,0:T(4,128)S(1)} %copy-done.3, f32[1,5,5]{2,0,1:T(1,128)S(1)} %get-tuple-element.176), kind=kOutput, calls=%fused_computation.85 | convolution fusion | flops 2539595 | bytes 688228 | tf_op jit(solution)/shard_map/wv,tvabe->twabe/dot_general | solution.py:84
  333.2 2.5 copy.397
  340.0 4.0 %fusion.18 = f32[4,320,128]{2,1,0:T(8,128)} fusion(f32[4,320,128]{2,1,0:T(8,128)S(1)} %fusion.19, f32[4,320,320]{2,1,0:T(8,128)S(1)} %copy-done, f32[4,320,128]{2,1,0:T(8,128)S(1)} %copy-done.15, f32[4,320,128]{2,1,0:T(8,128)} %bitcast.461, f32[4,320,128]{2,1,0:T(8,128)} %copy.403), kind=kOutput, calls=%fused_computation.53 | convolution fusion | flops 629637120 | bytes 4915200 | tf_op jit(solution)/shard_map/tpq,tqe->tpe/dot_general | solution.py:157
  (166 shorter events, 93.3 us)
Async XLA Ops:
  0.6 172.4 %copy-start = (f32[4,320,320]{2,1,0:T(8,128)S(1)}, f32[4,320,320]{2,1,0:T(8,128)}, u32[]{:S(2)}) copy-start(f32[4,320,320]{2,1,0:T(8,128)} %param.38) | copy-start | bytes 4915204
  0.6 22.0 %copy-start.28 = (f32[4,4,1,1,1,1]{1,0,5,4,3,2:T(4,128)S(1)}, f32[4,4,1,1,1,1]{1,0,5,4,3,2:T(4,128)}, u32[]{:S(2)}) copy-start(f32[4,4,1,1,1,1]{1,0,5,4,3,2:T(4,128)} %constant.421) | copy-start | bytes 196
  0.7 14.7 %copy-start.1 = (f32[4,320,128]{2,1,0:T(8,128)S(1)}, f32[4,320,128]{2,1,0:T(8,128)}, u32[]{:S(2)}) copy-start(f32[4,320,128]{2,1,0:T(8,128)} %param.35) | copy-start | bytes 1966084
  6.7 21.4 %copy-start.29 = (s32[4,1,64]{2,1,0:T(1,128)S(1)}, s32[4,1,64]{2,1,0:T(1,128)}, u32[]{:S(2)}) copy-start(s32[4,1,64]{2,1,0:T(1,128)} %param.40) | copy-start | bytes 3076
  7.5 111.2 %collective-permute-start.1 = (f32[4,80,64]{2,1,0:T(8,128)}, f32[4,80,64]{2,1,0:T(8,128)}, u32[]{:S(2)}, u32[]{:S(2)}) collective-permute-start(f32[4,80,64]{2,1,0:T(8,128)} %select_bitcast_fusion.1), channel_id=1, source_target_pairs={{1,0},{2,1},{3,2},{5,4},{6,5},{7,6},{9,8},{10,9},{11,10},{13,12},{... | collective-permute-start | bytes 245768 | tf_op jit(solution)/shard_map/ppermute | solution.py:25
  10.1 18.8 %copy-start.31 = (s32[4,64]{1,0:T(4,128)S(1)}, s32[4,64]{1,0:T(4,128)}, u32[]{:S(2)}) copy-start(s32[4,64]{1,0:T(4,128)} %param.39) | copy-start | bytes 3076
  10.9 104.0 %collective-permute-start = (f32[4,80,64]{1,2,0:T(8,128)}, f32[4,80,64]{1,2,0:T(8,128)S(1)}, u32[]{:S(2)}, u32[]{:S(2)}) collective-permute-start(f32[4,80,64]{1,2,0:T(8,128)} %copy.324), channel_id=1, source_target_pairs={{0,1},{1,2},{2,3},{4,5},{5,6},{6,7},{8,9},{9,10},{10,11},{12,13},{... | collective-permute-start | bytes 245768 | tf_op jit(solution)/shard_map/ppermute | solution.py:22
  16.5 116.3 %all-to-all-start = ((f32[4,320,128]{1,0,2:T(4,128)}), f32[4,320,128]{1,0,2:T(4,128)}, u32[]{:S(2)}, u32[]{:S(2)}) async-start(f32[4,320,128]{1,0,2:T(4,128)} %copy.355), calls=%async_computation | async-start | bytes 1572864 | tf_op jit(solution)/shard_map/all_to_all | solution.py:70
  30.4 8.8 %copy-start.30 = (f32[3,5,5]{2,0,1:T(4,128)S(1)}, f32[3,5,5]{2,0,1:T(4,128)}, u32[]{:S(2)}) copy-start(f32[3,5,5]{2,0,1:T(4,128)} %param.37) | copy-start | bytes 904
  45.5 1.0 copy-start.10
  46.5 8.9 %copy-start.20 = (f32[4,5,4,4,128]{4,3,2,1,0:T(4,128)S(1)}, f32[4,5,4,4,128]{4,3,2,1,0:T(4,128)}, u32[]{:S(2)}) copy-start(f32[4,5,4,4,128]{4,3,2,1,0:T(4,128)} %get-tuple-element.161) | copy-start | bytes 491524
  51.1 7.5 %copy-start.19 = (f32[4,5,4,4,1,128]{5,4,3,2,1,0:T(1,128)S(1)}, f32[4,5,4,4,1,128]{5,4,3,2,1,0:T(1,128)}, u32[]{:S(2)}) copy-start(f32[4,5,4,4,1,128]{5,4,3,2,1,0:T(1,128)} %get-tuple-element.159) | copy-start | bytes 491524
  98.8 5.9 %copy-start.9 = (f32[4,5,4,1,4,128]{1,4,2,0,5,3:T(4,128)S(1)}, f32[4,5,4,1,4,128]{1,4,2,0,5,3:T(4,128)}, u32[]{:S(2)}) copy-start(f32[4,5,4,1,4,128]{1,4,2,0,5,3:T(4,128)} %copy.451) | copy-start | bytes 491524
  98.8 7.4 %copy-start.12 = (f32[128,4,5,4,4]{2,4,3,1,0:T(4,128)S(1)}, f32[128,4,5,4,4]{2,4,3,1,0:T(4,128)}, u32[]{:S(2)}) copy-start(f32[128,4,5,4,4]{2,4,3,1,0:T(4,128)} %gather_fusion.2) | copy-start | bytes 491524
  106.3 3.1 copy-start.7
  106.3 5.0 %copy-start.13 = (f32[128,4,5,4,4]{2,4,3,1,0:T(4,128)S(1)}, f32[128,4,5,4,4]{2,4,3,1,0:T(4,128)}, u32[]{:S(2)}) copy-start(f32[128,4,5,4,4]{2,4,3,1,0:T(4,128)} %gather_fusion.4) | copy-start | bytes 491524
  111.3 7.4 %copy-start.24 = (f32[4,5,1,4,4,64]{5,4,3,1,0,2:T(4,128)S(1)}, f32[4,5,1,4,4,64]{5,4,3,1,0,2:T(4,128)}, u32[]{:S(2)}) copy-start(f32[4,5,1,4,4,64]{5,4,3,1,0,2:T(4,128)} %get-tuple-element.172) | copy-start | bytes 245764
  111.3 7.4 %copy-start.25 = (f32[4,5,1,4,4,64]{5,4,3,1,0,2:T(4,128)S(1)}, f32[4,5,1,4,4,64]{5,4,3,1,0,2:T(4,128)}, u32[]{:S(2)}) copy-start(f32[4,5,1,4,4,64]{5,4,3,1,0,2:T(4,128)} %get-tuple-element.175) | copy-start | bytes 245764
  117.5 6.7 %copy-start.8 = (f32[4,5,4,4,128]{1,3,2,0,4:T(4,128)S(1)}, f32[4,5,4,4,128]{1,3,2,0,4:T(4,128)}, u32[]{:S(2)}) copy-start(f32[4,5,4,4,128]{1,3,2,0,4:T(4,128)} %bitcast_subtract_fusion.7) | copy-start | bytes 491524
  139.1 30.2 %all-to-all-start.1 = ((f32[32,320,16]{1,2,0:T(8,128)}), f32[32,320,16]{1,2,0:T(8,128)S(1)}, u32[]{:S(2)}, u32[]{:S(2)}) async-start(f32[32,320,16]{1,2,0:T(8,128)} %copy.358), calls=%async_computation.1 | async-start | bytes 1572864 | tf_op jit(solution)/shard_map/all_to_all | solution.py:69
  144.7 16.7 %copy-start.4 = (f32[4,5,4,4,128]{1,3,4,2,0:T(4,128)S(1)}, f32[4,5,4,4,128]{1,3,4,2,0:T(4,128)}, u32[]{:S(2)}) copy-start(f32[4,5,4,4,128]{1,3,4,2,0:T(4,128)} %bitcast_subtract_fusion.4) | copy-start | bytes 491524
  173.0 8.2 %copy-start.16 = (f32[4,320,128]{2,1,0:T(8,128)}, f32[4,320,128]{2,1,0:T(8,128)S(1)}, u32[]{:S(2)}) copy-start(f32[4,320,128]{2,1,0:T(8,128)S(1)} %add_subtract_fusion) | copy-start | bytes 1966084
  189.6 11.9 %copy-start.17 = (f32[4,5,4,4,128]{4,3,2,1,0:T(4,128)S(1)}, f32[4,5,4,4,128]{4,3,2,1,0:T(4,128)}, u32[]{:S(2)}) copy-start(f32[4,5,4,4,128]{4,3,2,1,0:T(4,128)} %get-tuple-element.158) | copy-start | bytes 491524
  193.1 12.9 %copy-start.23 = (f32[4,5,4,1,4,128]{5,4,3,2,1,0:T(4,128)S(1)}, f32[4,5,4,1,4,128]{5,4,3,2,1,0:T(4,128)}, u32[]{:S(2)}) copy-start(f32[4,5,4,1,4,128]{5,4,3,2,1,0:T(4,128)} %get-tuple-element.153) | copy-start | bytes 491524
  193.1 16.7 %copy-start.22 = (f32[4,5,4,1,4,128]{5,4,3,2,1,0:T(4,128)S(1)}, f32[4,5,4,1,4,128]{5,4,3,2,1,0:T(4,128)}, u32[]{:S(2)}) copy-start(f32[4,5,4,1,4,128]{5,4,3,2,1,0:T(4,128)} %get-tuple-element.154) | copy-start | bytes 491524
  199.3 86.3 %collective-permute-start.3 = (f32[4,80,64]{2,1,0:T(8,128)}, f32[4,80,64]{2,1,0:T(8,128)}, u32[]{:S(2)}, u32[]{:S(2)}) collective-permute-start(f32[4,80,64]{2,1,0:T(8,128)} %select_bitcast_fusion), channel_id=1, source_target_pairs={{1,0},{2,1},{3,2},{5,4},{6,5},{7,6},{9,8},{10,9},{11,10},{13,12},{... | collective-permute-start | bytes 245768 | tf_op jit(solution)/shard_map/ppermute | solution.py:25
  202.3 81.3 %collective-permute-start.2 = (f32[4,80,64]{1,2,0:T(8,128)S(1)}, f32[4,80,64]{1,2,0:T(8,128)S(1)}, u32[]{:S(2)}, u32[]{:S(2)}) collective-permute-start(f32[4,80,64]{1,2,0:T(8,128)S(1)} %copy.370), channel_id=1, source_target_pairs={{0,1},{1,2},{2,3},{4,5},{5,6},{6,7},{8,9},{9,10},{10,11},{12,13},{... | collective-permute-start | bytes 245768 | tf_op jit(solution)/shard_map/ppermute | solution.py:22
  206.0 14.7 %copy-start.21 = (f32[4,5,4,4,128]{4,3,2,1,0:T(4,128)S(1)}, f32[4,5,4,4,128]{4,3,2,1,0:T(4,128)}, u32[]{:S(2)}) copy-start(f32[4,5,4,4,128]{4,3,2,1,0:T(4,128)} %get-tuple-element.152) | copy-start | bytes 491524
  231.5 5.8 %copy-start.18 = (f32[4,5,4,4,1,128]{5,4,3,2,1,0:T(1,128)S(1)}, f32[4,5,4,4,1,128]{5,4,3,2,1,0:T(1,128)}, u32[]{:S(2)}) copy-start(f32[4,5,4,4,1,128]{5,4,3,2,1,0:T(1,128)} %get-tuple-element.150) | copy-start | bytes 491524
  261.9 29.1 %all-to-all-start.2 = ((f32[4,320,128]{1,0,2:T(4,128)}), f32[4,320,128]{1,0,2:T(4,128)}, u32[]{:S(2)}, u32[]{:S(2)}) async-start(f32[4,320,128]{1,0,2:T(4,128)} %copy.398), calls=%async_computation.2 | async-start | bytes 1572864 | tf_op jit(solution)/shard_map/all_to_all | solution.py:70
  270.7 5.9 %copy-start.5 = (f32[4,5,4,4,1,128]{1,3,2,0,5,4:T(4,128)S(1)}, f32[4,5,4,4,1,128]{1,3,2,0,5,4:T(4,128)}, u32[]{:S(2)}) copy-start(f32[4,5,4,4,1,128]{1,3,2,0,5,4:T(4,128)} %copy.461) | copy-start | bytes 491524
  270.7 7.4 %copy-start.11 = (f32[128,4,5,4,4]{2,4,3,1,0:T(4,128)S(1)}, f32[128,4,5,4,4]{2,4,3,1,0:T(4,128)}, u32[]{:S(2)}) copy-start(f32[128,4,5,4,4]{2,4,3,1,0:T(4,128)} %gather_fusion.10) | copy-start | bytes 491524
  278.1 3.1 copy-start.14
  281.2 4.5 %copy-start.26 = (f32[4,5,1,4,4,64]{5,4,3,1,0,2:T(4,128)S(1)}, f32[4,5,1,4,4,64]{5,4,3,1,0,2:T(4,128)}, u32[]{:S(2)}) copy-start(f32[4,5,1,4,4,64]{5,4,3,1,0,2:T(4,128)} %get-tuple-element.168) | copy-start | bytes 245764
  281.2 4.5 %copy-start.27 = (f32[4,5,1,4,4,64]{5,4,3,1,0,2:T(4,128)S(1)}, f32[4,5,1,4,4,64]{5,4,3,1,0,2:T(4,128)}, u32[]{:S(2)}) copy-start(f32[4,5,1,4,4,64]{5,4,3,1,0,2:T(4,128)} %get-tuple-element.171) | copy-start | bytes 245764
  299.2 36.4 %all-to-all-start.3 = ((f32[32,320,16]{1,2,0:T(8,128)}), f32[32,320,16]{1,2,0:T(8,128)}, u32[]{:S(2)}, u32[]{:S(2)}) async-start(f32[32,320,16]{1,2,0:T(8,128)} %copy.401), calls=%async_computation.3 | async-start | bytes 1572864 | tf_op jit(solution)/shard_map/all_to_all | solution.py:69
  305.1 9.1 %copy-start.2 = (f32[4,5,4,4,128]{1,3,4,2,0:T(4,128)S(1)}, f32[4,5,4,4,128]{1,3,4,2,0:T(4,128)}, u32[]{:S(2)}) copy-start(f32[4,5,4,4,128]{1,3,4,2,0:T(4,128)} %bitcast_subtract_fusion.2) | copy-start | bytes 491524
  305.1 14.7 %copy-start.6 = (f32[4,5,4,4,128]{1,3,2,0,4:T(4,128)S(1)}, f32[4,5,4,4,128]{1,3,2,0,4:T(4,128)}, u32[]{:S(2)}) copy-start(f32[4,5,4,4,128]{1,3,2,0,4:T(4,128)} %bitcast_subtract_fusion.1) | copy-start | bytes 491524
  314.2 13.5 %copy-start.3 = (f32[4,5,4,4,128]{1,3,4,2,0:T(4,128)S(1)}, f32[4,5,4,4,128]{1,3,4,2,0:T(4,128)}, u32[]{:S(2)}) copy-start(f32[4,5,4,4,128]{1,3,4,2,0:T(4,128)} %bitcast_subtract_fusion) | copy-start | bytes 491524
  327.7 12.3 %copy-start.15 = (f32[4,320,128]{2,1,0:T(8,128)S(1)}, f32[4,320,128]{2,1,0:T(8,128)}, u32[]{:S(2)}) copy-start(f32[4,320,128]{2,1,0:T(8,128)} %param.36) | copy-start | bytes 1966084
where the time goes:
time: 349 us; the launch traced here: 344 us
  local copies, waits for them, and re-layouts  162 us (46%)
  matrix products  97.3 us (28%)
  other arithmetic  47.5 us (14%)
  starting transfers between devices  35.7 us (10%)
    dot_general x12, matrix products, face_term(): jnp.einsum('wv,tvabe->twabe', matrix, plus - minus, precision=lax.Precisi...  62.8 us
    unnamed x80, local copies, waits for them, and re-layouts  43.1 us
    sub x10, other arithmetic, face_term(): plus - minus  41.5 us
    gather x2, local copies, waits for them, and re-layouts, space_residual(): jnp.take(high_z, neighbours[2], axis=4)  15.5 us
    gather x2, local copies, waits for them, and re-layouts, space_residual(): jnp.take(low_y, neighbours[1], axis=4)  15.5 us
    gather x2, local copies, waits for them, and re-layouts, space_residual(): jnp.take(low_z, neighbours[3], axis=4)  15.5 us
    gather x2, local copies, waits for them, and re-layouts, space_residual(): jnp.take(high_y, neighbours[0], axis=4)  15.4 us
    all_to_all x2, starting transfers between devices, time_rates(): lax.all_to_all(field, 'inst', split_axis=2, concat_axis=0, tiled=True)  12.1 us
  transfers between devices with their start and end apart: 8, of which 0 were waited for; matrix products, arithmetic and copies ran while one was open for 70% of the time, Pallas kernels for 0%

commit v1 on v0

--- a/solution.py
+++ b/solution.py
@@ -12,6 +12,13 @@
 SWEEPS = 2
 dissipation = 0.6
 frequency = 0.25
+
+
+def stacked_exchange(array, name, split, join):
+    size = lax.axis_size(name)
+    pieces = jnp.stack(jnp.split(array, size, axis=split), axis=0)
+    pieces = lax.all_to_all(pieces, name, split_axis=0, concat_axis=0)
+    return jnp.concatenate(pieces, axis=join)
 
 
 def with_halo(block, sides, width):
@@ -67,7 +74,7 @@
 
 def time_rates(field):
     return lax.all_to_all(
-        differentiate(lax.all_to_all(field, "inst", split_axis=2, concat_axis=0, tiled=True)),
+        differentiate(stacked_exchange(field, "inst", 2, 0)),
         "inst",
         split_axis=0,
         concat_axis=2,

time: 349 us -> 387 us (1.11)
  local copies, waits for them, and re-layouts: 162 us -> 198 us
    unnamed x80 -> x103, local copies, waits for them, and re-layouts: 43.1 us -> 68.6 us
    another operation x0 -> x11, local copies, waits for them, and re-layouts: none -> 16.3 us  [stacked_exchange(): pieces = jnp.stack(jnp.split(array, size, axis=split), axis=0)]
    all_to_all x10 -> x4, local copies, waits for them, and re-layouts: 14.4 us -> 6.71 us  [time_rates(): lax.all_to_all(differentiate(stacked_exchange(field, 'inst', 2, 0)), 'ins...]
  transfers between devices with their start and end apart: 8 -> 8, of which waited for: 0 -> 0; matrix products, arithmetic and copies ran while one was open for 70% -> 75% of each run, Pallas kernels for 0% -> 0%
where the time goes in v1:
time: 387 us; the launch traced here: 380 us
  local copies, waits for them, and re-layouts  198 us (51%)
  matrix products  97.5 us (25%)
  other arithmetic  47.4 us (12%)
  starting transfers between devices  35.7 us (9%)
    unnamed x103, local copies, waits for them, and re-layouts  68.6 us
    dot_general x12, matrix products, face_term(): jnp.einsum('wv,tvabe->twabe', matrix, plus - minus, precision=lax.Precisi...  62.7 us
    sub x10, other arithmetic, face_term(): plus - minus  41.4 us
    another operation x11, local copies, waits for them, and re-layouts, stacked_exchange(): pieces = jnp.stack(jnp.split(array, size, axis=split), axis=0)  16.3 us
    gather x2, local copies, waits for them, and re-layouts, space_residual(): jnp.take(high_y, neighbours[0], axis=4)  15.5 us
    gather x2, local copies, waits for them, and re-layouts, space_residual(): jnp.take(high_z, neighbours[2], axis=4)  15.5 us
    gather x2, local copies, waits for them, and re-layouts, space_residual(): jnp.take(low_z, neighbours[3], axis=4)  15.4 us
    gather x2, local copies, waits for them, and re-layouts, space_residual(): jnp.take(low_y, neighbours[1], axis=4)  15.4 us
  transfers between devices with their start and end apart: 8, of which 0 were waited for; matrix products, arithmetic and copies ran while one was open for 75% of the time, Pallas kernels for 0%

profile of v1, /device:TPU:1, one launch (start us, length us, event | category | flops | bytes accessed | tf_op | source)
XLA Modules:
  0.0 380.0 jit_solution(8829340700310710376)
XLA Ops:
  10.8 4.5 %collective-permute-start = (f32[4,80,64]{1,2,0:T(8,128)}, f32[4,80,64]{1,2,0:T(8,128)S(1)}, u32[]{:S(2)}, u32[]{:S(2)}) collective-permute-start(f32[4,80,64]{1,2,0:T(8,128)} %copy.332), channel_id=1, source_target_pairs={{0,1},{1,2},{2,3},{4,5},{5,6},{6,7},{8,9},{9,10},{10,11},{12,13},{... | collective-permute-start | bytes 245768 | tf_op jit(solution)/shard_map/ppermute | solution.py:29
  15.3 3.4 fusion.289
  42.5 6.1 %all-to-all-start = ((f32[8,4,320,16]{2,3,1,0:T(8,128)}), f32[8,4,320,16]{2,3,1,0:T(8,128)}, u32[]{:S(2)}, u32[]{:S(2)}) async-start(f32[8,4,320,16]{2,3,1,0:T(8,128)} %bitcast_dynamic-update-slice_fusion), calls=%async_computation | async-start | bytes 1572864 | tf_op jit(solution)/shard_map/all_to_all | solution.py:20
  56.4 4.4 %copy.477 = f32[4,5,4,4,1,128]{1,3,2,0,5,4:T(4,128)} copy(f32[4,5,4,4,1,128]{5,4,3,2,1,0:T(1,128)} %get-tuple-element.176) | data formatting | bytes 327680
  60.8 4.3 %copy.493 = f32[4,5,4,4,1,128]{1,3,5,2,0,4:T(4,128)} copy(f32[4,5,4,4,1,128]{5,4,3,2,1,0:T(1,128)} %get-tuple-element.176) | data formatting | bytes 327680 | tf_op jit(solution)/shard_map/squeeze | solution.py:125
  67.6 2.4 convolution_add_fusion.3
  72.4 4.6 %copy.473 = f32[4,5,4,1,4,128]{1,4,2,0,5,3:T(4,128)} copy(f32[4,5,4,1,4,128]{5,4,3,2,1,0:T(4,128)} %get-tuple-element.178) | data formatting | bytes 327680
  76.9 4.3 %copy.472 = f32[4,5,4,1,4,128]{1,4,5,2,0,3:T(4,128)} copy(f32[4,5,4,1,4,128]{5,4,3,2,1,0:T(4,128)} %get-tuple-element.179) | data formatting | bytes 327680
  81.3 3.2 copy.350
  84.5 3.3 copy.476
  87.8 7.7 %gather_fusion.2 = f32[128,4,5,4,4]{2,4,3,1,0:T(4,128)} fusion(f32[4,5,4,4,128]{1,3,4,2,0:T(4,128)} %bitcast.472, s32[1024]{0:T(1024)S(1)} %pad_clamp_fusion.3), kind=kCustom, calls=%fused_computation.1.clone | custom fusion | bytes 328192 | tf_op jit(solution)/shard_map/jit(_take)/gather | solution.py:132
  95.5 7.7 %gather_fusion.3 = f32[128,4,5,4,4]{2,4,3,1,0:T(4,128)} fusion(f32[4,5,4,4,128]{1,3,4,2,0:T(4,128)} %copy.350, s32[1024]{0:T(1024)S(1)} %pad_clamp_fusion.2), kind=kCustom, calls=%fused_computation.5.clone | custom fusion | bytes 328192 | tf_op jit(solution)/shard_map/jit(_take)/gather | solution.py:135
  103.2 6.0 %bitcast_subtract_fusion.6 = f32[4,5,4,4,128]{1,3,4,2,0:T(4,128)} fusion(f32[128,4,5,4,4]{2,4,3,1,0:T(4,128)} %gather_fusion.3, pred[128]{0:T(512)(128)(4,1)S(1)} %get-tuple-element.205, f32[4,5,4,1,4,128]{1,4,5,2,0,3:T(4,128)} %copy.472), kind=kLoop, calls=%fused_computation.22 | loop fusion | flops 81920 | bytes 491648 | tf_op jit(solution)/shard_map/sub | solution.py:91
  109.2 7.8 %gather_fusion.4 = f32[128,4,5,4,4]{2,4,3,1,0:T(4,128)} fusion(f32[4,5,4,4,128]{1,3,4,2,0:T(4,128)} %bitcast.473, s32[1024]{0:T(1024)S(1)} %pad_clamp_fusion.1), kind=kCustom, calls=%fused_computation.6.clone | custom fusion | bytes 328192 | tf_op jit(solution)/shard_map/jit(_take)/gather | solution.py:138
  116.9 7.7 %gather_fusion.5 = f32[128,4,5,4,4]{2,4,3,1,0:T(4,128)} fusion(f32[4,5,4,4,128]{1,3,4,2,0:T(4,128)} %bitcast.477, s32[1024]{0:T(1024)S(1)} %pad_clamp_fusion), kind=kCustom, calls=%fused_computation.7.clone | custom fusion | bytes 328192 | tf_op jit(solution)/shard_map/jit(_take)/gather | solution.py:141
  124.6 5.9 %bitcast_subtract_fusion.4 = f32[4,5,4,4,128]{1,3,4,2,0:T(4,128)} fusion(f32[128,4,5,4,4]{2,4,3,1,0:T(4,128)} %gather_fusion.5, pred[128]{0:T(512)(128)(4,1)S(1)} %get-tuple-element.203, f32[4,5,4,4,1,128]{1,3,5,2,0,4:T(4,128)} %copy.476), kind=kLoop, calls=%fused_computation.20 | loop fusion | flops 81920 | bytes 491648 | tf_op jit(solution)/shard_map/sub | solution.py:91
  132.1 3.1 bitcast_subtract_fusion.7
  137.1 3.5 bitcast_subtract_fusion.5
  150.0 6.9 %fusion.126 = f32[4,5,4,4,4,128]{5,1,4,3,2,0:T(8,128)} fusion(f32[4,5,4,4,4,128]{5,1,4,3,2,0:T(8,128)} %fusion.134, f32[4,5,4,1,4,128]{5,1,4,2,0,3:T(8,128)S(1)} %slice_bitcast_fusion.10, f32[4,5,4,4,128]{1,3,2,0,4:T(4,128)S(1)} %copy-done.8, f32[1,5,5]{2,0,1:T(1,128)S(1)} %get-tuple-element.193), kind=kOutput, calls=%fused_computation.98 | convolution fusion | flops 2539620 | bytes 589924 | tf_op jit(solution)/shard_map/wv,tvabe->twabe/dot_general | solution.py:91
  162.1 5.6 %all-to-all-start.1 = ((f32[32,320,16]{1,2,0:T(8,128)}), f32[32,320,16]{1,2,0:T(8,128)S(1)}, u32[]{:S(2)}, u32[]{:S(2)}) async-start(f32[32,320,16]{1,2,0:T(8,128)} %copy.372), calls=%async_computation.1 | async-start | bytes 1572864 | tf_op jit(solution)/shard_map/all_to_all | solution.py:76
  167.7 6.8 %fusion.117 = f32[4,5,4,4,4,128]{5,1,4,3,2,0:T(8,128)} fusion(f32[4,5,4,4,4,128]{5,1,4,3,2,0:T(8,128)} %fusion.126, f32[4,5,4,1,4,128]{5,1,4,2,0,3:T(8,128)} %slice_bitcast_fusion.9, f32[4,5,4,4,128]{1,3,4,2,0:T(4,128)} %bitcast_subtract_fusion.6, f32[1,5,5]{2,0,1:T(1,128)S(1)} %get-tuple-element.193), kind=kOutput, calls=%fused_computation.95 | convolution fusion | flops 2539595 | bytes 4718692 | tf_op jit(solution)/shard_map/wv,tvabe->twabe/dot_general | solution.py:91
  175.5 8.9 %fusion.108 = f32[4,5,4,4,4,128]{5,1,4,3,2,0:T(8,128)} fusion(f32[4,5,4,4,4,128]{5,1,4,3,2,0:T(8,128)} %fusion.117, f32[4,5,4,4,1,128]{5,1,3,2,0,4:T(8,128)S(1)} %slice_bitcast_fusion.8, f32[4,5,4,4,128]{1,3,2,0,4:T(4,128)} %bitcast_subtract_fusion.5, f32[1,5,5]{2,0,1:T(1,128)S(1)} %get-tuple-element.192), kind=kOutput, calls=%fused_computation.92 | convolution fusion | flops 2539620 | bytes 4620388 | tf_op jit(solution)/shard_map/wv,tvabe->twabe/dot_general | solution.py:91
  184.4 5.7 %fusion.99 = f32[4,5,4,4,4,128]{5,1,4,3,2,0:T(8,128)} fusion(f32[4,5,4,4,4,128]{5,1,4,3,2,0:T(8,128)} %fusion.108, f32[4,5,4,4,128]{1,3,4,2,0:T(4,128)S(1)} %copy-done.5, f32[1,5,5]{2,0,1:T(1,128)S(1)} %get-tuple-element.192), kind=kOutput, calls=%fused_computation.89 | convolution fusion | flops 2539595 | bytes 688228 | tf_op jit(solution)/shard_map/wv,tvabe->twabe/dot_general | solution.py:91
  206.1 3.3 copy.491
  209.4 3.1 copy.495
  212.5 3.5 slice_bitcast_fusion
  227.2 3.7 collective-permute-start.2
  230.9 3.8 %copy.489 = f32[4,5,4,1,4,128]{1,4,2,0,5,3:T(4,128)} copy(f32[4,5,4,1,4,128]{5,4,3,2,1,0:T(4,128)S(1)} %copy-done.24) | data formatting | bytes 327680
  234.7 3.2 copy.488
  237.9 7.8 %gather_fusion.8 = f32[128,4,5,4,4]{2,4,3,1,0:T(4,128)} fusion(f32[4,5,4,4,128]{1,3,4,2,0:T(4,128)} %bitcast.474, s32[1024]{0:T(1024)S(1)} %pad_clamp_fusion.3), kind=kCustom, calls=%fused_computation.8.clone | custom fusion | bytes 328192 | tf_op jit(solution)/shard_map/jit(_take)/gather | solution.py:132
  245.7 3.1 copy.400
  248.8 7.7 %gather_fusion.9 = f32[128,4,5,4,4]{2,4,3,1,0:T(4,128)} fusion(f32[4,5,4,4,128]{1,3,4,2,0:T(4,128)} %copy.400, s32[1024]{0:T(1024)S(1)} %pad_clamp_fusion.2), kind=kCustom, calls=%fused_computation.9.clone | custom fusion | bytes 328192 | tf_op jit(solution)/shard_map/jit(_take)/gather | solution.py:135
  256.5 5.8 %bitcast_subtract_fusion.2 = f32[4,5,4,4,128]{1,3,4,2,0:T(4,128)} fusion(f32[128,4,5,4,4]{2,4,3,1,0:T(4,128)} %gather_fusion.9, pred[128]{0:T(512)(128)(4,1)S(1)} %get-tuple-element.205, f32[4,5,4,1,4,128]{1,4,5,2,0,3:T(4,128)} %copy.488), kind=kLoop, calls=%fused_computation.16 | loop fusion | flops 81920 | bytes 491648 | tf_op jit(solution)/shard_map/sub | solution.py:91
  262.3 3.3 copy.490
  265.5 7.7 %gather_fusion.10 = f32[128,4,5,4,4]{2,4,3,1,0:T(4,128)} fusion(f32[4,5,4,4,128]{1,3,4,2,0:T(4,128)} %bitcast.475, s32[1024]{0:T(1024)S(1)} %pad_clamp_fusion.1), kind=kCustom, calls=%fused_computation.10.clone | custom fusion | bytes 328192 | tf_op jit(solution)/shard_map/jit(_take)/gather | solution.py:138
  273.2 7.7 %gather_fusion.11 = f32[128,4,5,4,4]{2,4,3,1,0:T(4,128)} fusion(f32[4,5,4,4,128]{1,3,4,2,0:T(4,128)} %bitcast.476, s32[1024]{0:T(1024)S(1)} %pad_clamp_fusion), kind=kCustom, calls=%fused_computation.11.clone | custom fusion | bytes 328192 | tf_op jit(solution)/shard_map/jit(_take)/gather | solution.py:141
  281.0 5.8 %bitcast_subtract_fusion = f32[4,5,4,4,128]{1,3,4,2,0:T(4,128)} fusion(f32[128,4,5,4,4]{2,4,3,1,0:T(4,128)} %gather_fusion.11, pred[128]{0:T(512)(128)(4,1)S(1)} %get-tuple-element.203, f32[4,5,4,4,1,128]{1,3,5,2,0,4:T(4,128)} %copy.490), kind=kLoop, calls=%fused_computation.12 | loop fusion | flops 81920 | bytes 491648 | tf_op jit(solution)/shard_map/sub | solution.py:91
  302.5 6.0 %all-to-all-start.2 = ((f32[8,4,320,16]{2,3,1,0:T(8,128)}), f32[8,4,320,16]{2,3,1,0:T(8,128)}, u32[]{:S(2)}, u32[]{:S(2)}) async-start(f32[8,4,320,16]{2,3,1,0:T(8,128)} %constant_dynamic-update-slice_fusion), calls=%async_computation.2 | async-start | bytes 1572864 | tf_op jit(solution)/shard_map/all_to_all | solution.py:20
  308.5 2.8 convolution_add_fusion.1
  311.3 5.8 %bitcast_subtract_fusion.3 = f32[4,5,4,4,128]{1,3,2,0,4:T(4,128)} fusion(f32[4,5,4,1,4,128]{1,4,2,0,5,3:T(4,128)} %copy.489, f32[128,4,5,4,4]{2,4,3,1,0:T(4,128)} %gather_fusion.8, pred[128]{0:T(512)(128)(4,1)S(1)} %get-tuple-element.206), kind=kLoop, calls=%fused_computation.19 | loop fusion | flops 81920 | bytes 491648 | tf_op jit(solution)/shard_map/sub | solution.py:91
  318.7 3.1 bitcast_subtract_fusion.1
  335.0 5.8 %all-to-all-start.3 = ((f32[32,320,16]{1,2,0:T(8,128)}), f32[32,320,16]{1,2,0:T(8,128)}, u32[]{:S(2)}, u32[]{:S(2)}) async-start(f32[32,320,16]{1,2,0:T(8,128)} %copy.421), calls=%async_computation.3 | async-start | bytes 1572864 | tf_op jit(solution)/shard_map/all_to_all | solution.py:76
  340.8 9.1 %fusion.81 = f32[4,5,4,4,4,128]{5,1,3,2,0,4:T(8,128)} fusion(f32[4,5,4,4,4,128]{5,1,3,2,0,4:T(8,128)} %fusion.138, f32[4,5,4,4,128]{1,3,2,0,4:T(4,128)} %bitcast_subtract_fusion.3, f32[1,5,5]{2,0,1:T(1,128)S(1)} %get-tuple-element.193), kind=kOutput, calls=%fused_computation.83 | convolution fusion | flops 2539620 | bytes 4718692 | tf_op jit(solution)/shard_map/wv,tvabe->twabe/dot_general | solution.py:91
  349.9 5.6 %fusion.75 = f32[4,5,4,4,4,128]{5,1,3,2,0,4:T(8,128)} fusion(f32[4,5,4,4,4,128]{5,1,3,2,0,4:T(8,128)} %fusion.81, f32[4,5,4,4,128]{1,3,4,2,0:T(4,128)S(1)} %copy-done.2, f32[1,5,5]{2,0,1:T(1,128)S(1)} %get-tuple-element.193), kind=kOutput, calls=%fused_computation.81 | convolution fusion | flops 2539595 | bytes 688228 | tf_op jit(solution)/shard_map/wv,tvabe->twabe/dot_general | solution.py:91
  355.5 7.9 %fusion.93 = f32[4,5,4,4,4,128]{5,1,3,2,0,4:T(8,128)} fusion(f32[4,5,4,4,4,128]{5,1,3,2,0,4:T(8,128)} %fusion.75, f32[4,5,4,4,128]{1,3,2,0,4:T(4,128)S(1)} %copy-done.6, f32[1,5,5]{2,0,1:T(1,128)S(1)} %get-tuple-element.192), kind=kOutput, calls=%fused_computation.87 | convolution fusion | flops 2539620 | bytes 688228 | tf_op jit(solution)/shard_map/wv,tvabe->twabe/dot_general | solution.py:91
  363.4 5.5 %fusion.87 = f32[4,5,4,4,4,128]{5,1,3,2,0,4:T(8,128)} fusion(f32[4,5,4,4,4,128]{5,1,3,2,0,4:T(8,128)} %fusion.93, f32[4,5,4,4,128]{1,3,4,2,0:T(4,128)S(1)} %copy-done.4, f32[1,5,5]{2,0,1:T(1,128)S(1)} %get-tuple-element.192), kind=kOutput, calls=%fused_computation.85 | convolution fusion | flops 2539595 | bytes 688228 | tf_op jit(solution)/shard_map/wv,tvabe->twabe/dot_general | solution.py:91
  368.9 2.5 copy.411
  375.8 4.0 %fusion.18 = f32[4,320,128]{2,1,0:T(8,128)} fusion(f32[4,320,128]{2,1,0:T(8,128)S(1)} %fusion.19, f32[4,320,320]{2,1,0:T(8,128)S(1)} %copy-done, f32[4,320,128]{2,1,0:T(8,128)S(1)} %copy-done.15, f32[4,320,128]{2,1,0:T(8,128)} %bitcast.481, f32[4,320,128]{2,1,0:T(8,128)} %copy.423), kind=kOutput, calls=%fused_computation.53 | convolution fusion | flops 629637120 | bytes 4915200 | tf_op jit(solution)/shard_map/tpq,tqe->tpe/dot_general | solution.py:164
  (194 shorter events, 127.4 us)
Async XLA Ops:
  0.6 195.5 %copy-start = (f32[4,320,320]{2,1,0:T(8,128)S(1)}, f32[4,320,320]{2,1,0:T(8,128)}, u32[]{:S(2)}) copy-start(f32[4,320,320]{2,1,0:T(8,128)} %param.38) | copy-start | bytes 4915204
  0.6 14.7 %copy-start.1 = (f32[4,320,128]{2,1,0:T(8,128)S(1)}, f32[4,320,128]{2,1,0:T(8,128)}, u32[]{:S(2)}) copy-start(f32[4,320,128]{2,1,0:T(8,128)} %param.35) | copy-start | bytes 1966084
  7.4 137.0 %collective-permute-start.1 = (f32[4,80,64]{2,1,0:T(8,128)}, f32[4,80,64]{2,1,0:T(8,128)}, u32[]{:S(2)}, u32[]{:S(2)}) collective-permute-start(f32[4,80,64]{2,1,0:T(8,128)} %select_bitcast_fusion.1), channel_id=1, source_target_pairs={{1,0},{2,1},{3,2},{5,4},{6,5},{7,6},{9,8},{10,9},{11,10},{13,12},{... | collective-permute-start | bytes 245768 | tf_op jit(solution)/shard_map/ppermute | solution.py:32
  10.8 129.8 %collective-permute-start = (f32[4,80,64]{1,2,0:T(8,128)}, f32[4,80,64]{1,2,0:T(8,128)S(1)}, u32[]{:S(2)}, u32[]{:S(2)}) collective-permute-start(f32[4,80,64]{1,2,0:T(8,128)} %copy.332), channel_id=1, source_target_pairs={{0,1},{1,2},{2,3},{4,5},{5,6},{6,7},{8,9},{9,10},{10,11},{12,13},{... | collective-permute-start | bytes 245768 | tf_op jit(solution)/shard_map/ppermute | solution.py:29
  20.0 28.7 %copy-start.29 = (f32[4,4,1,1,1,1]{1,0,5,4,3,2:T(4,128)S(1)}, f32[4,4,1,1,1,1]{1,0,5,4,3,2:T(4,128)}, u32[]{:S(2)}) copy-start(f32[4,4,1,1,1,1]{1,0,5,4,3,2:T(4,128)} %constant.421) | copy-start | bytes 196
  30.5 23.6 %copy-start.30 = (s32[4,1,64]{2,1,0:T(1,128)S(1)}, s32[4,1,64]{2,1,0:T(1,128)}, u32[]{:S(2)}) copy-start(s32[4,1,64]{2,1,0:T(1,128)} %param.40) | copy-start | bytes 3076
  31.8 23.1 %copy-start.32 = (s32[4,64]{1,0:T(4,128)S(1)}, s32[4,64]{1,0:T(4,128)}, u32[]{:S(2)}) copy-start(s32[4,64]{1,0:T(4,128)} %param.39) | copy-start | bytes 3076
  42.5 116.1 %all-to-all-start = ((f32[8,4,320,16]{2,3,1,0:T(8,128)}), f32[8,4,320,16]{2,3,1,0:T(8,128)}, u32[]{:S(2)}, u32[]{:S(2)}) async-start(f32[8,4,320,16]{2,3,1,0:T(8,128)} %bitcast_dynamic-update-slice_fusion), calls=%async_computation | async-start | bytes 1572864 | tf_op jit(solution)/shard_map/all_to_all | solution.py:20
  56.4 8.7 %copy-start.31 = (f32[3,5,5]{2,0,1:T(4,128)S(1)}, f32[3,5,5]{2,0,1:T(4,128)}, u32[]{:S(2)}) copy-start(f32[3,5,5]{2,0,1:T(4,128)} %param.37) | copy-start | bytes 904
  71.4 1.0 copy-start.10
  72.4 8.9 %copy-start.21 = (f32[4,5,4,4,128]{4,3,2,1,0:T(4,128)S(1)}, f32[4,5,4,4,128]{4,3,2,1,0:T(4,128)}, u32[]{:S(2)}) copy-start(f32[4,5,4,4,128]{4,3,2,1,0:T(4,128)} %get-tuple-element.177) | copy-start | bytes 491524
  76.9 7.5 %copy-start.20 = (f32[4,5,4,4,1,128]{5,4,3,2,1,0:T(1,128)S(1)}, f32[4,5,4,4,1,128]{5,4,3,2,1,0:T(1,128)}, u32[]{:S(2)}) copy-start(f32[4,5,4,4,1,128]{5,4,3,2,1,0:T(1,128)} %get-tuple-element.175) | copy-start | bytes 491524
  124.6 5.9 %copy-start.9 = (f32[4,5,4,1,4,128]{1,4,2,0,5,3:T(4,128)S(1)}, f32[4,5,4,1,4,128]{1,4,2,0,5,3:T(4,128)}, u32[]{:S(2)}) copy-start(f32[4,5,4,1,4,128]{1,4,2,0,5,3:T(4,128)} %copy.473) | copy-start | bytes 491524
  124.6 7.4 %copy-start.12 = (f32[128,4,5,4,4]{2,4,3,1,0:T(4,128)S(1)}, f32[128,4,5,4,4]{2,4,3,1,0:T(4,128)}, u32[]{:S(2)}) copy-start(f32[128,4,5,4,4]{2,4,3,1,0:T(4,128)} %gather_fusion.2) | copy-start | bytes 491524
  132.1 3.1 copy-start.7
  132.1 5.0 %copy-start.13 = (f32[128,4,5,4,4]{2,4,3,1,0:T(4,128)S(1)}, f32[128,4,5,4,4]{2,4,3,1,0:T(4,128)}, u32[]{:S(2)}) copy-start(f32[128,4,5,4,4]{2,4,3,1,0:T(4,128)} %gather_fusion.4) | copy-start | bytes 491524
  137.1 7.4 %copy-start.25 = (f32[4,5,1,4,4,64]{5,4,3,1,0,2:T(4,128)S(1)}, f32[4,5,1,4,4,64]{5,4,3,1,0,2:T(4,128)}, u32[]{:S(2)}) copy-start(f32[4,5,1,4,4,64]{5,4,3,1,0,2:T(4,128)} %get-tuple-element.188) | copy-start | bytes 245764
  137.1 7.4 %copy-start.26 = (f32[4,5,1,4,4,64]{5,4,3,1,0,2:T(4,128)S(1)}, f32[4,5,1,4,4,64]{5,4,3,1,0,2:T(4,128)}, u32[]{:S(2)}) copy-start(f32[4,5,1,4,4,64]{5,4,3,1,0,2:T(4,128)} %get-tuple-element.191) | copy-start | bytes 245764
  143.3 6.7 %copy-start.8 = (f32[4,5,4,4,128]{1,3,2,0,4:T(4,128)S(1)}, f32[4,5,4,4,128]{1,3,2,0,4:T(4,128)}, u32[]{:S(2)}) copy-start(f32[4,5,4,4,128]{1,3,2,0,4:T(4,128)} %bitcast_subtract_fusion.7) | copy-start | bytes 491524
  162.1 30.2 %all-to-all-start.1 = ((f32[32,320,16]{1,2,0:T(8,128)}), f32[32,320,16]{1,2,0:T(8,128)S(1)}, u32[]{:S(2)}, u32[]{:S(2)}) async-start(f32[32,320,16]{1,2,0:T(8,128)} %copy.372), calls=%async_computation.1 | async-start | bytes 1572864 | tf_op jit(solution)/shard_map/all_to_all | solution.py:76
  167.7 16.7 %copy-start.5 = (f32[4,5,4,4,128]{1,3,4,2,0:T(4,128)S(1)}, f32[4,5,4,4,128]{1,3,4,2,0:T(4,128)}, u32[]{:S(2)}) copy-start(f32[4,5,4,4,128]{1,3,4,2,0:T(4,128)} %bitcast_subtract_fusion.4) | copy-start | bytes 491524
  196.1 8.2 %copy-start.16 = (f32[4,320,128]{2,1,0:T(8,128)}, f32[4,320,128]{2,1,0:T(8,128)S(1)}, u32[]{:S(2)}) copy-start(f32[4,320,128]{2,1,0:T(8,128)S(1)} %add_subtract_fusion) | copy-start | bytes 1966084
  212.5 5.9 %copy-start.18 = (f32[4,5,4,4,128]{4,3,2,1,0:T(4,128)S(1)}, f32[4,5,4,4,128]{4,3,2,1,0:T(4,128)}, u32[]{:S(2)}) copy-start(f32[4,5,4,4,128]{4,3,2,1,0:T(4,128)} %get-tuple-element.165) | copy-start | bytes 491524
  216.0 9.7 %copy-start.17 = (f32[4,5,4,4,128]{4,3,2,1,0:T(4,128)S(1)}, f32[4,5,4,4,128]{4,3,2,1,0:T(4,128)}, u32[]{:S(2)}) copy-start(f32[4,5,4,4,128]{4,3,2,1,0:T(4,128)} %get-tuple-element.166) | copy-start | bytes 491524
  218.4 12.5 %copy-start.24 = (f32[4,5,4,1,4,128]{5,4,3,2,1,0:T(4,128)S(1)}, f32[4,5,4,1,4,128]{5,4,3,2,1,0:T(4,128)}, u32[]{:S(2)}) copy-start(f32[4,5,4,1,4,128]{5,4,3,2,1,0:T(4,128)} %get-tuple-element.161) | copy-start | bytes 491524
  218.4 16.3 %copy-start.23 = (f32[4,5,4,1,4,128]{5,4,3,2,1,0:T(4,128)S(1)}, f32[4,5,4,1,4,128]{5,4,3,2,1,0:T(4,128)}, u32[]{:S(2)}) copy-start(f32[4,5,4,1,4,128]{5,4,3,2,1,0:T(4,128)} %get-tuple-element.162) | copy-start | bytes 491524
  223.6 102.6 %collective-permute-start.3 = (f32[4,80,64]{2,1,0:T(8,128)}, f32[4,80,64]{2,1,0:T(8,128)}, u32[]{:S(2)}, u32[]{:S(2)}) collective-permute-start(f32[4,80,64]{2,1,0:T(8,128)} %select_bitcast_fusion), channel_id=1, source_target_pairs={{1,0},{2,1},{3,2},{5,4},{6,5},{7,6},{9,8},{10,9},{11,10},{13,12},{... | collective-permute-start | bytes 245768 | tf_op jit(solution)/shard_map/ppermute | solution.py:32
  227.2 96.9 %collective-permute-start.2 = (f32[4,80,64]{1,2,0:T(8,128)}, f32[4,80,64]{1,2,0:T(8,128)S(1)}, u32[]{:S(2)}, u32[]{:S(2)}) collective-permute-start(f32[4,80,64]{1,2,0:T(8,128)} %copy.384), channel_id=1, source_target_pairs={{0,1},{1,2},{2,3},{4,5},{5,6},{6,7},{8,9},{9,10},{10,11},{12,13},{... | collective-permute-start | bytes 245768 | tf_op jit(solution)/shard_map/ppermute | solution.py:29
  230.8 14.8 %copy-start.22 = (f32[4,5,4,4,128]{4,3,2,1,0:T(4,128)S(1)}, f32[4,5,4,4,128]{4,3,2,1,0:T(4,128)}, u32[]{:S(2)}) copy-start(f32[4,5,4,4,128]{4,3,2,1,0:T(4,128)} %get-tuple-element.160) | copy-start | bytes 491524
  256.5 5.8 %copy-start.19 = (f32[4,5,4,4,1,128]{5,4,3,2,1,0:T(1,128)S(1)}, f32[4,5,4,4,1,128]{5,4,3,2,1,0:T(1,128)}, u32[]{:S(2)}) copy-start(f32[4,5,4,4,1,128]{5,4,3,2,1,0:T(1,128)} %get-tuple-element.158) | copy-start | bytes 491524
  302.5 29.0 %all-to-all-start.2 = ((f32[8,4,320,16]{2,3,1,0:T(8,128)}), f32[8,4,320,16]{2,3,1,0:T(8,128)}, u32[]{:S(2)}, u32[]{:S(2)}) async-start(f32[8,4,320,16]{2,3,1,0:T(8,128)} %constant_dynamic-update-slice_fusion), calls=%async_computation.2 | async-start | bytes 1572864 | tf_op jit(solution)/shard_map/all_to_all | solution.py:20
  311.2 5.8 %copy-start.3 = (f32[4,5,4,4,1,128]{1,3,2,0,5,4:T(4,128)S(1)}, f32[4,5,4,4,1,128]{1,3,2,0,5,4:T(4,128)}, u32[]{:S(2)}) copy-start(f32[4,5,4,4,1,128]{1,3,2,0,5,4:T(4,128)} %copy.491) | copy-start | bytes 491524
  311.3 7.4 %copy-start.11 = (f32[128,4,5,4,4]{2,4,3,1,0:T(4,128)S(1)}, f32[128,4,5,4,4]{2,4,3,1,0:T(4,128)}, u32[]{:S(2)}) copy-start(f32[128,4,5,4,4]{2,4,3,1,0:T(4,128)} %gather_fusion.10) | copy-start | bytes 491524
  318.7 3.1 copy-start.14
  321.8 4.4 %copy-start.27 = (f32[4,5,1,4,4,64]{5,4,3,1,0,2:T(4,128)S(1)}, f32[4,5,1,4,4,64]{5,4,3,1,0,2:T(4,128)}, u32[]{:S(2)}) copy-start(f32[4,5,1,4,4,64]{5,4,3,1,0,2:T(4,128)} %get-tuple-element.184) | copy-start | bytes 245764
  321.8 4.4 %copy-start.28 = (f32[4,5,1,4,4,64]{5,4,3,1,0,2:T(4,128)S(1)}, f32[4,5,1,4,4,64]{5,4,3,1,0,2:T(4,128)}, u32[]{:S(2)}) copy-start(f32[4,5,1,4,4,64]{5,4,3,1,0,2:T(4,128)} %get-tuple-element.187) | copy-start | bytes 245764
  335.0 36.5 %all-to-all-start.3 = ((f32[32,320,16]{1,2,0:T(8,128)}), f32[32,320,16]{1,2,0:T(8,128)}, u32[]{:S(2)}, u32[]{:S(2)}) async-start(f32[32,320,16]{1,2,0:T(8,128)} %copy.421), calls=%async_computation.3 | async-start | bytes 1572864 | tf_op jit(solution)/shard_map/all_to_all | solution.py:76
  340.8 9.1 %copy-start.2 = (f32[4,5,4,4,128]{1,3,4,2,0:T(4,128)S(1)}, f32[4,5,4,4,128]{1,3,4,2,0:T(4,128)}, u32[]{:S(2)}) copy-start(f32[4,5,4,4,128]{1,3,4,2,0:T(4,128)} %bitcast_subtract_fusion.2) | copy-start | bytes 491524
  340.8 14.7 %copy-start.6 = (f32[4,5,4,4,128]{1,3,2,0,4:T(4,128)S(1)}, f32[4,5,4,4,128]{1,3,2,0,4:T(4,128)}, u32[]{:S(2)}) copy-start(f32[4,5,4,4,128]{1,3,2,0,4:T(4,128)} %bitcast_subtract_fusion.1) | copy-start | bytes 491524
  349.9 13.5 %copy-start.4 = (f32[4,5,4,4,128]{1,3,4,2,0:T(4,128)S(1)}, f32[4,5,4,4,128]{1,3,4,2,0:T(4,128)}, u32[]{:S(2)}) copy-start(f32[4,5,4,4,128]{1,3,4,2,0:T(4,128)} %bitcast_subtract_fusion) | copy-start | bytes 491524
  363.4 12.4 %copy-start.15 = (f32[4,320,128]{2,1,0:T(8,128)S(1)}, f32[4,320,128]{2,1,0:T(8,128)}, u32[]{:S(2)}) copy-start(f32[4,320,128]{2,1,0:T(8,128)} %param.36) | copy-start | bytes 1966084
